TPU v7x, 32 devices: a whole 2x2x4 slice. The times are simulated.
32 devices in a mesh: shard: 8 (over z, x), rep: 4 (over y, core).
Axes of the slice: x: 2, y: 2, z: 4, core: 2. Of those that a mesh axis runs over, the one named last changes fastest.
Arguments:
- tokens_in: float32 [31520, 768], P(('shard', 'rep')), may hold values from -6 to 6
- routes: int32 [31520, 2], P(('shard', 'rep')), may hold values from 0 to 3, all different within a row; in each aligned block of 985 rows (0 to 984, 985 to 1969, ...) at most 616 rows name the same one
- first_gain: bfloat16 [768], P('shard'), may hold values from 0.5 to 1.5
- first_shift: bfloat16 [768], P('shard'), may hold values from -3 to 3
- joint_weight: bfloat16 [768, 2304], P('shard'), may hold values from -0.21875 to 0.21875
- joint_bias: bfloat16 [2, 768], P(None, 'shard'), may hold values from -3 to 3
- mixer_weight: bfloat16 [768, 768], P('shard'), may hold values from -0.625 to 0.625
- mixer_bias: bfloat16 [768], P('shard'), may hold values from -3 to 3
- second_gain: bfloat16 [768], P('shard'), may hold values from 0.5 to 1.5
- second_shift: bfloat16 [768], P('shard'), may hold values from -3 to 3
- router_weight: bfloat16 [768, 4], P('shard'), may hold values from -0.4375 to 0.4375
- expert_up: bfloat16 [4, 768, 3072], P(None, None, 'shard'), may hold values from -0.21875 to 0.21875
- upward_bias: bfloat16 [4, 3072], P(None, 'shard'), may hold values from -3 to 3
- expert_down: bfloat16 [4, 3072, 768], P(None, 'shard'), may hold values from -0.3125 to 0.3125
- downward_bias: bfloat16 [4, 768], P(None, 'shard'), may hold values from -3 to 3
- out_grad: float32 [31520, 768], P(('shard', 'rep')), may hold values from -6 to 6
Outputs:
- block_out: float32 [31520, 768], P(('shard', 'rep'))
- input_grad: float32 [31520, 768], P(('shard', 'rep'))
- first_gain_grad: float32 [768], P('shard')
- first_shift_grad: float32 [768], P('shard')
- joint_weight_grad: float32 [768, 2304], P('shard')
- joint_bias_grad: float32 [2, 768], P(None, 'shard')
- mixer_weight_grad: float32 [768, 768], P('shard')
- mixer_bias_grad: float32 [768], P('shard')
- second_gain_grad: float32 [768], P('shard')
- second_shift_grad: float32 [768], P('shard')
- router_weight_grad: float32 [768, 4], P('shard')
- expert_up_grad: float32 [4, 768, 3072], P(None, None, 'shard')
- upward_bias_grad: float32 [4, 3072], P(None, 'shard')
- expert_down_grad: float32 [4, 3072, 768], P(None, 'shard')
- downward_bias_grad: float32 [4, 768], P(None, 'shard')
Inputs may be any that keep to these rules, and one draw needn't show every extreme that they name: `routes`: the two experts of a token differ. Among the rows of one device (985 aligned rows), no expert is named more than 616 times.
All inputs are finite; a program needn't handle non-finite values.
Results may differ from a plain program's by a relative error of at most 0.02.
Values may be sent and summed in bfloat16 or wider, within the bound.
A program may use at most 320 MiB of HBM per device.

v0:
```python
import jax
import jax.numpy as jnp
from jax import lax
from jax.sharding import PartitionSpec as P

HEADS = 12
HEAD_DIM = 64
SEQ = 197
CAP = 616
epsilon = 1e-06


def layer_norm(values, gain, shift):
    centre = jnp.mean(values, axis=-1, keepdims=True)
    centred = values - centre
    spread = jnp.mean(centred * centred, axis=-1, keepdims=True)
    factor = lax.rsqrt(spread + epsilon)
    unit_rows = centred * factor
    return (unit_rows * gain + shift, unit_rows, factor)


def norm_back(upstream, unit_rows, factor, gain):
    scaled = upstream * gain
    middle = jnp.mean(scaled, axis=-1, keepdims=True)
    along = jnp.mean(scaled * unit_rows, axis=-1, keepdims=True)
    return factor * (scaled - middle - unit_rows * along)


def gelu_slope(hidden):
    normal_cdf = 0.5 * (1.0 + lax.erf(hidden * 0.7071067811865476))
    density = jnp.exp(-0.5 * hidden * hidden) * 0.3989422804014327
    return normal_cdf + hidden * density


def contract_first(left_rows, right_rows):
    return lax.dot_general(
        left_rows, right_rows, (((0,), (0,)), ((), ())), preferred_element_type=jnp.float32
    )


def contract_last(left_rows, right_rows):
    return lax.dot_general(
        left_rows, right_rows, (((1,), (1,)), ((), ())), preferred_element_type=jnp.float32
    )


def dispatch_tables(routes, experts, capacity):
    token_count = routes.shape[0]
    flat_routes = routes.reshape(-1)
    hit_table = (flat_routes[:, None] == jnp.arange(experts, dtype=jnp.int32)[None, :]).astype(
        jnp.int32
    )
    earlier = jnp.cumsum(hit_table, axis=0) - hit_table
    slot_index = jnp.sum(earlier * hit_table, axis=1)
    position = flat_routes * capacity + slot_index
    entries = jnp.arange(2 * token_count, dtype=jnp.int32)
    owner = jnp.full((experts * capacity,), 2 * token_count, jnp.int32).at[position].set(entries)
    return (position, owner)


def shards(
    tokens_in,
    routes,
    first_gain,
    first_shift,
    joint_weight,
    joint_bias,
    mixer_weight,
    mixer_bias,
    second_gain,
    second_shift,
    router_weight,
    expert_up,
    upward_bias,
    expert_down,
    downward_bias,
    out_grad,
):
    token_count, width = tokens_in.shape
    experts = expert_up.shape[0]
    images = token_count // SEQ
    capacity = CAP
    head_scale = HEAD_DIM ** (-0.5)
    gathered = (
        lax.all_gather(first_gain, "shard", axis=0, tiled=True),
        lax.all_gather(first_shift, "shard", axis=0, tiled=True),
        lax.all_gather(joint_weight, "shard", axis=0, tiled=True),
        lax.all_gather(joint_bias, "shard", axis=1, tiled=True),
        lax.all_gather(mixer_weight, "shard", axis=0, tiled=True),
        lax.all_gather(mixer_bias, "shard", axis=0, tiled=True),
        lax.all_gather(second_gain, "shard", axis=0, tiled=True),
        lax.all_gather(second_shift, "shard", axis=0, tiled=True),
        lax.all_gather(router_weight, "shard", axis=0, tiled=True),
        lax.all_gather(downward_bias, "shard", axis=1, tiled=True),
    )
    (
        gain_one,
        shift_one,
        joint_full,
        joint_shift,
        mixer_full,
        mixer_shift,
        gain_two,
        shift_two,
        router_full,
        down_shift,
    ) = gathered
    gain_one = gain_one.astype(jnp.float32)
    gain_two = gain_two.astype(jnp.float32)
    down_shift = down_shift.astype(jnp.float32)
    normed_one, unit_one, factor_one = layer_norm(
        tokens_in, gain_one, shift_one.astype(jnp.float32)
    )
    normed_one = normed_one.astype(jnp.bfloat16)
    joint_shift = joint_shift.astype(jnp.float32)
    shift_all = jnp.concatenate([joint_shift[0], jnp.zeros((width,), jnp.float32), joint_shift[1]])
    projected = (
        jnp.dot(normed_one, joint_full, preferred_element_type=jnp.float32) + shift_all
    ).astype(jnp.bfloat16)
    parted = projected.reshape(images, SEQ, 3, HEADS, HEAD_DIM)
    queries = parted[:, :, 0]
    key_rows = parted[:, :, 1]
    value_rows = parted[:, :, 2]
    scores = (
        jnp.einsum("bqhd,bkhd->bhqk", queries, key_rows, preferred_element_type=jnp.float32)
        * head_scale
    )
    highest_score = jnp.max(scores, axis=-1, keepdims=True)
    log_total = highest_score + jnp.log(
        jnp.sum(jnp.exp(scores - highest_score), axis=-1, keepdims=True)
    )
    attention = jnp.exp(scores - log_total).astype(jnp.bfloat16)
    mixed = jnp.einsum("bhqk,bkhd->bqhd", attention, value_rows, preferred_element_type=jnp.float32)
    mixed = mixed.reshape(token_count, width).astype(jnp.bfloat16)
    residual_one = tokens_in + (
        jnp.dot(mixed, mixer_full, preferred_element_type=jnp.float32)
        + mixer_shift.astype(jnp.float32)
    )
    normed_two, unit_two, factor_two = layer_norm(
        residual_one, gain_two, shift_two.astype(jnp.float32)
    )
    normed_two = normed_two.astype(jnp.bfloat16)
    logits = jnp.dot(normed_two, router_full, preferred_element_type=jnp.float32)
    router_probs = jax.nn.softmax(logits, axis=-1)
    position, owner = dispatch_tables(routes, experts, capacity)
    choose = (routes[:, :, None] == jnp.arange(experts, dtype=jnp.int32)[None, None, :]).astype(
        jnp.float32
    )
    gates = jnp.sum(choose * router_probs[:, None, :], axis=-1)
    padded = jnp.concatenate([normed_two, jnp.zeros((1, width), jnp.bfloat16)], axis=0)
    dispatched = padded[owner // 2].reshape(experts, capacity, width)
    up_full, up_shift, down_full = (
        lax.all_gather(expert_up, "shard", axis=2, tiled=True),
        lax.all_gather(upward_bias, "shard", axis=1, tiled=True),
        lax.all_gather(expert_down, "shard", axis=1, tiled=True),
    )
    hidden = (
        jnp.einsum("ecd,edf->ecf", dispatched, up_full, preferred_element_type=jnp.float32)
        + up_shift.astype(jnp.float32)[:, None, :]
    )
    active = jax.nn.gelu(hidden, approximate=False).astype(jnp.bfloat16)
    expert_result = (
        jnp.einsum("ecf,efd->ecd", active, down_full, preferred_element_type=jnp.float32)
        + down_shift[:, None, :]
    )
    picked = expert_result.reshape(experts * capacity, width)[position].reshape(
        token_count, 2, width
    )
    block_out = residual_one + jnp.sum(gates[:, :, None] * picked, axis=1)
    gate_pad = jnp.concatenate([gates.reshape(-1), jnp.zeros((1,), jnp.float32)])
    grad_pad = jnp.concatenate([out_grad, jnp.zeros((1, width), jnp.float32)], axis=0)
    result_grad = (
        (gate_pad[owner][:, None] * grad_pad[owner // 2])
        .astype(jnp.bfloat16)
        .reshape(experts, capacity, width)
    )
    gate_grad = jnp.sum(out_grad[:, None, :] * picked, axis=-1)
    probs_grad = jnp.sum(choose * gate_grad[:, :, None], axis=1)
    logit_grad = (
        router_probs * (probs_grad - jnp.sum(router_probs * probs_grad, axis=-1, keepdims=True))
    ).astype(jnp.bfloat16)
    router_grad = contract_first(normed_two, logit_grad)
    normed_grad = contract_last(logit_grad, router_full)
    down_shift_grad = jnp.sum(result_grad.astype(jnp.float32), axis=1)
    up_full, down_full = (
        lax.all_gather(expert_up, "shard", axis=2, tiled=True),
        lax.all_gather(expert_down, "shard", axis=1, tiled=True),
    )
    active_grad = jnp.einsum(
        "ecd,efd->ecf", result_grad, down_full, preferred_element_type=jnp.float32
    )
    hidden_grad = (active_grad * gelu_slope(hidden)).astype(jnp.bfloat16)
    dispatched_grad = jnp.einsum(
        "ecf,edf->ecd", hidden_grad, up_full, preferred_element_type=jnp.float32
    )
    up_grad = jnp.einsum(
        "ecd,ecf->edf", dispatched, hidden_grad, preferred_element_type=jnp.float32
    )
    up_shift_grad = jnp.sum(hidden_grad.astype(jnp.float32), axis=1)
    down_grad = jnp.einsum("ecf,ecd->efd", active, result_grad, preferred_element_type=jnp.float32)
    up_grad, up_shift_grad, down_grad = (
        lax.psum_scatter(
            up_grad.astype(jnp.bfloat16), "shard", scatter_dimension=2, tiled=True
        ).astype(jnp.float32),
        lax.psum_scatter(
            up_shift_grad.astype(jnp.bfloat16), "shard", scatter_dimension=1, tiled=True
        ).astype(jnp.float32),
        lax.psum_scatter(
            down_grad.astype(jnp.bfloat16), "shard", scatter_dimension=1, tiled=True
        ).astype(jnp.float32),
    )
    routed_grad = dispatched_grad.reshape(experts * capacity, width)[position].reshape(
        token_count, 2, width
    )
    normed_grad = normed_grad + jnp.sum(routed_grad, axis=1)
    gain_two_grad = jnp.sum(normed_grad * unit_two, axis=0)
    shift_two_grad = jnp.sum(normed_grad, axis=0)
    residual_grad = out_grad + norm_back(normed_grad, unit_two, factor_two, gain_two)
    mixer_in_grad = residual_grad.astype(jnp.bfloat16)
    mixer_shift_grad = jnp.sum(mixer_in_grad.astype(jnp.float32), axis=0)
    joint_full, mixer_full = (
        lax.all_gather(joint_weight, "shard", axis=0, tiled=True),
        lax.all_gather(mixer_weight, "shard", axis=0, tiled=True),
    )
    mixer_grad = contract_first(mixed, mixer_in_grad)
    mixed_grad = (
        contract_last(mixer_in_grad, mixer_full)
        .astype(jnp.bfloat16)
        .reshape(images, SEQ, HEADS, HEAD_DIM)
    )
    scores_again = (
        jnp.einsum("bqhd,bkhd->bhqk", queries, key_rows, preferred_element_type=jnp.float32)
        * head_scale
    )
    attention_full = jnp.exp(scores_again - log_total)
    attention_low = attention_full.astype(jnp.bfloat16)
    weight_grad = jnp.einsum(
        "bqhd,bkhd->bhqk", mixed_grad, value_rows, preferred_element_type=jnp.float32
    )
    centre_grad = jnp.sum(attention_full * weight_grad, axis=-1, keepdims=True)
    score_grad = (attention_full * (weight_grad - centre_grad)).astype(jnp.bfloat16)
    query_grad = (
        jnp.einsum("bhqk,bkhd->bqhd", score_grad, key_rows, preferred_element_type=jnp.float32)
        * head_scale
    )
    key_grad = (
        jnp.einsum("bhqk,bqhd->bkhd", score_grad, queries, preferred_element_type=jnp.float32)
        * head_scale
    )
    value_grad = jnp.einsum(
        "bhqk,bqhd->bkhd", attention_low, mixed_grad, preferred_element_type=jnp.float32
    )
    projected_grad = (
        jnp.stack([query_grad, key_grad, value_grad], axis=2)
        .reshape(token_count, 3 * width)
        .astype(jnp.bfloat16)
    )
    joint_shift_grad = jnp.stack(
        [
            jnp.sum(projected_grad[:, :width].astype(jnp.float32), axis=0),
            jnp.sum(projected_grad[:, 2 * width :].astype(jnp.float32), axis=0),
        ]
    )
    joint_grad = contract_first(normed_one, projected_grad)
    first_grad = contract_last(projected_grad, joint_full)
    gain_one_grad = jnp.sum(first_grad * unit_one, axis=0)
    shift_one_grad = jnp.sum(first_grad, axis=0)
    input_grad = residual_grad + norm_back(first_grad, unit_one, factor_one, gain_one)
    group_sums = (
        lax.psum_scatter(
            gain_one_grad.astype(jnp.bfloat16), "shard", scatter_dimension=0, tiled=True
        ).astype(jnp.float32),
        lax.psum_scatter(
            shift_one_grad.astype(jnp.bfloat16), "shard", scatter_dimension=0, tiled=True
        ).astype(jnp.float32),
        lax.psum_scatter(
            joint_grad.astype(jnp.bfloat16), "shard", scatter_dimension=0, tiled=True
        ).astype(jnp.float32),
        lax.psum_scatter(
            joint_shift_grad.astype(jnp.bfloat16), "shard", scatter_dimension=1, tiled=True
        ).astype(jnp.float32),
        lax.psum_scatter(
            mixer_grad.astype(jnp.bfloat16), "shard", scatter_dimension=0, tiled=True
        ).astype(jnp.float32),
        lax.psum_scatter(
            mixer_shift_grad.astype(jnp.bfloat16), "shard", scatter_dimension=0, tiled=True
        ).astype(jnp.float32),
        lax.psum_scatter(
            gain_two_grad.astype(jnp.bfloat16), "shard", scatter_dimension=0, tiled=True
        ).astype(jnp.float32),
        lax.psum_scatter(
            shift_two_grad.astype(jnp.bfloat16), "shard", scatter_dimension=0, tiled=True
        ).astype(jnp.float32),
        lax.psum_scatter(
            router_grad.astype(jnp.bfloat16), "shard", scatter_dimension=0, tiled=True
        ).astype(jnp.float32),
        lax.psum_scatter(
            down_shift_grad.astype(jnp.bfloat16), "shard", scatter_dimension=1, tiled=True
        ).astype(jnp.float32),
    )
    (
        gain_one_grad,
        shift_one_grad,
        joint_grad,
        joint_shift_grad,
        mixer_grad,
        mixer_shift_grad,
        gain_two_grad,
        shift_two_grad,
        router_grad,
        down_shift_grad,
    ) = group_sums
    totals = (
        lax.psum(gain_one_grad.astype(jnp.bfloat16), "rep").astype(jnp.float32),
        lax.psum(shift_one_grad.astype(jnp.bfloat16), "rep").astype(jnp.float32),
        lax.psum(joint_grad.astype(jnp.bfloat16), "rep").astype(jnp.float32),
        lax.psum(joint_shift_grad.astype(jnp.bfloat16), "rep").astype(jnp.float32),
        lax.psum(mixer_grad.astype(jnp.bfloat16), "rep").astype(jnp.float32),
        lax.psum(mixer_shift_grad.astype(jnp.bfloat16), "rep").astype(jnp.float32),
        lax.psum(gain_two_grad.astype(jnp.bfloat16), "rep").astype(jnp.float32),
        lax.psum(shift_two_grad.astype(jnp.bfloat16), "rep").astype(jnp.float32),
        lax.psum(router_grad.astype(jnp.bfloat16), "rep").astype(jnp.float32),
        lax.psum(up_grad.astype(jnp.bfloat16), "rep").astype(jnp.float32),
        lax.psum(up_shift_grad.astype(jnp.bfloat16), "rep").astype(jnp.float32),
        lax.psum(down_grad.astype(jnp.bfloat16), "rep").astype(jnp.float32),
        lax.psum(down_shift_grad.astype(jnp.bfloat16), "rep").astype(jnp.float32),
    )
    return (
        block_out,
        input_grad,
        totals[0],
        totals[1],
        totals[2],
        totals[3],
        totals[4],
        totals[5],
        totals[6],
        totals[7],
        totals[8],
        totals[9],
        totals[10],
        totals[11],
        totals[12],
    )


def solution(mesh):
    placed = (
        P(("shard", "rep"), None),
        P(("shard", "rep"), None),
        P("shard"),
        P("shard"),
        P("shard", None),
        P(None, "shard"),
        P("shard", None),
        P("shard"),
        P("shard"),
        P("shard"),
        P("shard", None),
        P(None, None, "shard"),
        P(None, "shard"),
        P(None, "shard", None),
        P(None, "shard"),
        P(("shard", "rep"), None),
    )
    return jax.shard_map(
        shards,
        mesh=mesh,
        in_specs=placed,
        out_specs=(
            P(("shard", "rep"), None),
            P(("shard", "rep"), None),
            P("shard"),
            P("shard"),
            P("shard", None),
            P(None, "shard"),
            P("shard", None),
            P("shard"),
            P("shard"),
            P("shard"),
            P("shard", None),
            P(None, None, "shard"),
            P(None, "shard"),
            P(None, "shard", None),
            P(None, "shard"),
        ),
        check_vma=False,
    )
```

profile of v0, /device:TPU:0, one launch (start us, length us, event | category | flops | bytes accessed | tf_op | source)
XLA Modules:
  0.0 2104.7 jit_solution(18119825212157746471)
XLA Ops:
  16.2 40.6 %all-reduce.14 = (bf16[768]{0:T(1024)(128)(2,1)S(1)}, bf16[768]{0:T(1024)(128)(2,1)S(1)}, bf16[768]{0:T(1024)(128)(2,1)S(1)}, bf16[768]{0:T(1024)(128)(2,1)S(1)}, bf16[768]{0:T(1024)(128)(2,1)S(1)}) all-reduce(bf16[768]{0:T(1024)(128)(2,1)S(1)} %dynamic-update-slice.1, ...), channel_id=1, replica_groups=mesh['shard'=8,'rep'=4] {'shard'}, use_global_device_ids=true, to_apply=%add.4 | all-reduce | flops 3840 | bytes 15360
  59.8 16.8 all-gather
  77.2 18.5 all-gather.1
  96.4 31.0 %all_gather.53 = bf16[4,3072]{1,0:T(4,128)(2,1)S(1)} all-gather(bf16[4,384]{1,0:T(4,128)(2,1)} %param.28), channel_id=1, replica_groups=mesh['shard'=8,'rep'=4] {'shard'}, dimensions={1}, use_global_device_ids=true | all-gather | bytes 27648 | tf_op jit(solution)/shard_map/all_gather | solution.py:154
  139.6 10.5 scatter_custom_fusion
  150.2 8.4 gather_fusion.3
  161.1 9.0 add_convert_fusion
  170.2 14.6 reshape.294
  184.8 9.0 fusion.50
  193.9 6.0 copy.163
  199.9 6.1 copy.162
  206.0 5.2 copy.164
  211.2 4.1 multiply_reduce_fusion.1
  222.6 3.1 copy.129
  225.7 5.7 convert_element_type.190
  231.5 3.4 fusion.52
  239.7 13.3 gather_fusion.2
  253.2 8.5 gather_fusion
  261.6 5.5 fusion.49
  267.2 215.8 %all-gather.12.cloned.1.call-done = bf16[4,768,3072]{2,1,0:T(8,128)(2,1)} async-done(((bf16[4,768,384]{2,1,0:T(8,128)(2,1)}), bf16[4,768,3072]{2,1,0:T(8,128)(2,1)}) %all-gather.12.cloned.1.call-update) | async-done | bytes 18874384 | tf_op jit(solution)/shard_map/all_gather | solution.py:153
  482.9 29.5 %fusion.17 = (u8[616,3072]{1,0:T(8,128)(4,1)S(1)}, u8[616,3072]{1,0:T(8,128)(4,1)}, f32[4,616,3072]{2,1,0:T(8,128)}) fusion(f32[4,3072]{1,0:T(4,128)S(1)} %copy-done.24, bf16[4,616,768]{2,1,0:T(8,128)(2,1)} %bitcast.130, bf16[4,768,3072]{2,1,0:T(8,128)(2,1)} %all-gather.12.cloned.1.call-done), kind=kOutput, calls=%fused_computation.46 | convolution fusion | flops 11728797696 | bytes 56770560 | tf_op jit(solution)/shard_map/ecd,edf->ecf/dot_general | solution.py:158
  512.4 334.3 %all-gather.14.cloned.1.call-done = bf16[4,3072,768]{2,1,0:T(8,128)(2,1)} async-done(((bf16[4,384,768]{2,1,0:T(8,128)(2,1)}), bf16[4,3072,768]{2,1,0:T(8,128)(2,1)}) %all-gather.14.cloned.1.call-update) | async-done | bytes 18874384 | tf_op jit(solution)/shard_map/all_gather | solution.py:155
  846.7 30.4 %fusion.54 = (bf16[4,3072]{1,0:T(4,128)(2,1)}, bf16[4,616,3072]{2,1,0:T(8,128)(2,1)}) fusion(f32[4,616,3072]{2,1,0:T(8,128)} %get-tuple-element.72, f32[4,3072]{1,0:T(4,128)S(1)} %copy-done.24, bf16[4,616,768]{2,1,0:T(8,128)(2,1)} %get-tuple-element.55, bf16[4,3072,768]{2,1,0:T(8,128)(2,1)} %all-gather.14.cloned.1.call-done), kind=kOutput, calls=%fused_computation.148 | convolution fusion | flops 11717431296 | bytes 68149248 | tf_op jit(solution)/shard_map/ecd,efd->ecf/dot_general | solution.py:189
  877.1 23.7 %convolution_convert_fusion.1 = bf16[4,768,3072]{2,1,0:T(8,128)(2,1)} fusion(bf16[4,616,768]{2,1,0:T(8,128)(2,1)S(1)} %bitcast.131, bf16[4,616,3072]{2,1,0:T(8,128)(2,1)} %get-tuple-element.78), kind=kOutput, calls=%fused_computation.41 | convolution fusion | flops 11636047872 | bytes 37797888 | tf_op jit(solution)/shard_map/ecd,ecf->edf/dot_general | solution.py:196
  900.8 29.5 %copy.152 = bf16[4,768,3072]{1,0,2:T(4,128)(2,1)} copy(bf16[4,768,3072]{2,1,0:T(8,128)(2,1)} %convolution_convert_fusion.1) | data formatting | bytes 37748736
  930.2 20.0 copy.167
  950.9 20.0 all-gather.2
  971.0 20.1 fusion.55
  991.1 13.7 gather_fusion.4
  1004.8 8.2 reshape.192
  1013.0 11.6 reduce_sum.267
  1024.6 71.8 %fusion.2 = bf16[4,616,3072]{2,1,0:T(8,128)(2,1)} fusion(f32[4,616,3072]{2,1,0:T(8,128)} %get-tuple-element.72, f32[4,3072]{1,0:T(4,128)S(1)} %copy-done.24, u8[616,3072]{1,0:T(8,128)(4,1)} %get-tuple-element.16, u8[616,3072]{1,0:T(8,128)(4,1)S(1)} %get-tuple-element.15), kind=kLoop, calls=%fused_computation.10 | loop fusion | flops 537427968 | bytes 49250304 | tf_op jit(solution)/shard_map/convert_element_type | solution.py:161
  1096.3 21.0 broadcast_add_fusion
  1117.3 13.7 gather_fusion.1
  1131.0 8.0 reshape.189
  1139.0 17.2 multiply_reduce_fusion.2
  1159.7 5.4 multiply_reduce_fusion.4
  1169.7 4.4 reshape.295
  1174.1 6.0 copy.138
  1180.1 5.0 convolution_convert_fusion.4
  1185.1 8.6 multiply_reduce_fusion
  1193.7 6.9 multiply_convert_fusion
  1203.2 3.4 fusion.32
  1206.9 4.2 fusion.29
  1211.2 7.2 convert_bitcast_fusion
  1219.8 8.6 copy.143
  1228.4 14.0 convert_element_type.205
  1242.5 8.5 convolution_convert_fusion.2
  1251.4 21.8 %convolution_convert_fusion = bf16[4,3072,768]{2,1,0:T(8,128)(2,1)} fusion(bf16[4,616,3072]{2,1,0:T(8,128)(2,1)} %fusion.2, bf16[4,616,768]{2,1,0:T(8,128)(2,1)} %get-tuple-element.55), kind=kOutput, calls=%fused_computation.40 | convolution fusion | flops 11636047872 | bytes 37797888 | tf_op jit(solution)/shard_map/ecf,ecd->efd/dot_general | solution.py:200
  1282.3 5.6 reshape.284
  1287.9 5.4 copy.153
  1293.2 34.1 %reduce-scatter.21.cloned.1.call-done = bf16[96,768]{1,0:T(8,128)(2,1)} async-done(((bf16[768,768]{1,0:T(8,128)(2,1)}), bf16[96,768]{1,0:T(8,128)(2,1)}) %reduce-scatter.21.cloned.1.call-update) | async-done | bytes 147472 | tf_op jit(solution)/shard_map/reduce_scatter | solution.py:282
  1327.3 82.1 %reduce-scatter.19.cloned.1.call-done = bf16[96,2304]{1,0:T(8,128)(2,1)} async-done(((bf16[768,2304]{1,0:T(8,128)(2,1)}), bf16[96,2304]{1,0:T(8,128)(2,1)}) %reduce-scatter.19.cloned.1.call-update) | async-done | bytes 442384 | tf_op jit(solution)/shard_map/reduce_scatter | solution.py:276
  1409.4 313.2 %reduce-scatter.23.cloned.1.call-done = bf16[4,384,768]{2,1,0:T(8,128)(2,1)} async-done(((bf16[4,3072,768]{2,1,0:T(8,128)(2,1)}), bf16[4,384,768]{2,1,0:T(8,128)(2,1)}) %reduce-scatter.23.cloned.1.call-update) | async-done | bytes 2359312 | tf_op jit(solution)/shard_map/reduce_scatter | solution.py:208
  1723.3 63.7 %reduce-scatter.33.cloned.1.call-done = bf16[96,4]{1,0:T(8,128)(2,1)} async-done(((bf16[768,4]{1,0:T(8,128)(2,1)}), bf16[96,4]{1,0:T(8,128)(2,1)}) %reduce-scatter.33.cloned.1.call-update) | async-done | bytes 784
  1787.8 9.8 multiply_reduce_fusion.5
  1797.6 35.2 %all-reduce.13 = (bf16[768]{0:T(1024)(128)(2,1)S(1)}, bf16[768]{0:T(1024)(128)(2,1)S(1)}, bf16[768]{0:T(1024)(128)(2,1)S(1)}, bf16[768]{0:T(1024)(128)(2,1)S(1)}, bf16[768]{0:T(1024)(128)(2,1)S(1)}) all-reduce(bf16[768]{0:T(1024)(128)(2,1)S(1)} %get-tuple-element.19, ...), channel_id=2, replica_groups=mesh['shard'=8,'rep'=4] {'shard'}, use_global_device_ids=true, to_apply=%region_24.25.clone | all-reduce | flops 3840 | bytes 15360
  1833.1 4.4 multiply_add_fusion
  1837.6 14.2 reduce-scatter.25.cloned.1.call-done
  1852.6 63.5 %reduce-scatter.27.cloned.1.call-done = bf16[96,4]{1,0:T(8,128)(2,1)} async-done(((bf16[768,4]{1,0:T(8,128)(2,1)}), bf16[96,4]{1,0:T(8,128)(2,1)}) %reduce-scatter.27.cloned.1.call-update) | async-done | bytes 784
  1916.8 65.3 %reduce-scatter.31.cloned.1.call-done = bf16[384,4]{1,0:T(8,128)(2,1)} async-done(((bf16[3072,4]{1,0:T(8,128)(2,1)}), bf16[384,4]{1,0:T(8,128)(2,1)}) %reduce-scatter.31.cloned.1.call-update) | async-done | bytes 3088
  1983.1 5.8 all-reduce.15
  1993.8 93.7 %all-reduce.19.cloned.1.call-done = (bf16[96,2304]{1,0:T(8,128)(2,1)}, bf16[96,768]{1,0:T(8,128)(2,1)}, bf16[4,768,384]{2,1,0:T(8,128)(2,1)}, bf16[4,384,768]{2,1,0:T(8,128)(2,1)}) async-done(((bf16[96,2304]{1,0:T(8,128)(2,1)}, bf16[96,768]{1,0:T(8,128)(2,1)}, bf16[4,768,384]{2,1,0:T(8,128)(2,1)}, bf16[4,384,768]{2,1,0:T(8,128)(2,1)}), (bf16[96,2304]{1,0:T(8,128)(2,1)}, bf16[96,768]{1,0:T(8,128)(2,1)}, ...) | async-done | bytes 5308432 | tf_op jit(solution)/shard_map/psum | solution.py:316
  2091.3 4.2 convert_element_type.225
  (244 shorter events, 76.8 us)
Async XLA Ops:
  7.2 130.1 %copy-start.7 = (f32[985,768]{1,0:T(8,128)S(1)}, f32[985,768]{1,0:T(8,128)}, u32[]{:S(2)}) copy-start(f32[985,768]{1,0:T(8,128)} %param.16) | copy-start | bytes 9077764
  7.2 153.9 %all-gather.8.cloned.1.call-start = ((), (), s32[]{:S(2)}) async-start(), calls=%async_computation.8 | async-start | bytes 3981312 | tf_op jit(solution)/shard_map/all_gather | solution.py:87
  7.9 223.6 %all-gather.10.cloned.1.call-start = ((), (), s32[]{:S(2)}) async-start(), calls=%async_computation.9 | async-start | bytes 1327104 | tf_op jit(solution)/shard_map/all_gather | solution.py:89
  8.7 474.2 %all-gather.12.cloned.1.call-start = ((), (), s32[]{:S(2)}) async-start(), calls=%async_computation.10 | async-start | bytes 21233664 | tf_op jit(solution)/shard_map/all_gather | solution.py:153
  9.4 837.3 %all-gather.14.cloned.1.call-start = ((), (), s32[]{:S(2)}) async-start(), calls=%async_computation.11 | async-start | bytes 21233664 | tf_op jit(solution)/shard_map/all_gather | solution.py:155
  10.0 1272.3 %reduce-scatter.29.cloned.1.call-start = ((), (), s32[]{:S(2)}) async-start(), calls=%async_computation.17 | async-start | bytes 21233664
  134.8 4.8 copy-start.29
  134.8 4.8 copy-start.38
  139.6 10.5 copy-start.39
  150.2 8.5 copy-start.43
  150.2 10.9 copy-start.44
  150.2 10.9 copy-start.49
  158.7 11.5 copy-start.36
  161.1 9.1 copy-start.46
  211.1 4.1 copy-start.4
  215.3 4.8 copy-start
  215.3 4.8 copy-start.12
  220.1 2.5 copy-start.21
  222.6 8.9 copy-start.8
  222.6 8.9 copy-start.51
  231.5 5.1 copy-start.30
  231.5 5.1 copy-start.48
  234.9 1.6 copy-start.2
  234.9 2.2 copy-start.35
  234.9 3.4 copy-start.25
  234.9 2.8 copy-start.26
  236.5 1.2 copy-start.32
  237.1 16.0 copy-start.11
  238.5 0.8 copy-start.17
  261.6 221.3 %copy-start.24 = (f32[4,3072]{1,0:T(4,128)S(1)}, f32[4,3072]{1,0:T(4,128)}, u32[]{:S(2)}) copy-start(f32[4,3072]{1,0:T(4,128)} %convert_element_type.196) | copy-start | bytes 147460
  846.7 30.4 %copy-start.19 = (bf16[2464,768]{1,0:T(8,128)(2,1)S(1)}, bf16[2464,768]{1,0:T(8,128)(2,1)}, u32[]{:S(2)}) copy-start(bf16[2464,768]{1,0:T(8,128)(2,1)} %gather_fusion) | copy-start | bytes 11354116
  950.3 0.7 copy-start.52
  950.3 20.7 copy-start.40
  950.3 377.0 %reduce-scatter.21.cloned.1.call-start = ((), (), s32[]{:S(2)}) async-start(), calls=%async_computation.13 | async-start | bytes 1327104 | tf_op jit(solution)/shard_map/reduce_scatter | solution.py:282
  1131.0 8.0 copy-start.18
  1139.0 20.7 copy-start.3
  1159.7 5.5 copy-start.6
  1159.7 5.5 copy-start.27
  1159.7 5.5 copy-start.31
  1159.7 5.5 copy-start.33
  1165.2 3.0 copy-start.53
  1166.6 1.6 copy-start.15
  1180.1 5.0 copy-start.13
  1180.1 5.0 copy-start.22
  1193.7 9.5 copy-start.10
  1200.6 2.6 copy-start.1
  1203.2 3.7 copy-start.5
  1206.7 202.7 %reduce-scatter.19.cloned.1.call-start = ((), (), s32[]{:S(2)}) async-start(), calls=%async_computation.12 | async-start | bytes 3981312 | tf_op jit(solution)/shard_map/reduce_scatter | solution.py:276
  1206.9 4.2 copy-start.14
  1211.2 7.2 copy-start.16
  1228.4 14.0 copy-start.9
  1228.4 14.0 copy-start.37
  1228.4 14.0 copy-start.45
  1228.4 14.0 copy-start.47
  1228.4 14.0 copy-start.50
  1250.9 471.6 %reduce-scatter.23.cloned.1.call-start = ((), (), s32[]{:S(2)}) async-start(), calls=%async_computation.14 | async-start | bytes 21233664 | tf_op jit(solution)/shard_map/reduce_scatter | solution.py:208
  1273.2 0.7 copy-start.41
  1273.2 7.6 copy-start.42
  1273.2 513.8 %reduce-scatter.33.cloned.1.call-start = ((), (), s32[]{:S(2)}) async-start(), calls=%async_computation.19 | async-start | bytes 221184
  1274.7 577.0 %reduce-scatter.25.cloned.1.call-start = ((), (), s32[]{:S(2)}) async-start(), calls=%async_computation.15 | async-start | bytes 221184
  1278.1 637.9 %reduce-scatter.27.cloned.1.call-start = ((), (), s32[]{:S(2)}) async-start(), calls=%async_computation.16 | async-start | bytes 221184
  1280.7 701.4 %reduce-scatter.31.cloned.1.call-start = ((), (), s32[]{:S(2)}) async-start(), calls=%async_computation.18 | async-start | bytes 884736
  1282.0 805.4 %all-reduce.19.cloned.1.call-start = ((), (), s32[]{:S(2)}) async-start(), calls=%async_computation.20 | async-start | bytes 10616832 | tf_op jit(solution)/shard_map/psum | solution.py:316
  2087.5 7.9 copy-start.20
  (3 other events, 1.8 us)
Sparse Core Ops, SparseCore 0:
  10.2 67.7 all-gather.7
  80.2 40.0 all-gather.9
  121.8 361.0 all-gather.11
  484.3 362.3 all-gather.13
  950.4 309.7 reduce-scatter.28
  1263.5 63.7 reduce-scatter.20
  1331.0 78.4 reduce-scatter.18
  1413.3 309.2 reduce-scatter.22
  1725.8 61.0 reduce-scatter.32
  1790.7 61.0 reduce-scatter.24
  1855.0 60.9 reduce-scatter.26
  1919.7 62.3 reduce-scatter.30
  1984.8 102.6 all-reduce.18
where the time goes:
time: 2110 us; the launch traced here: 2100 us
  waiting for transfers between devices  1280 us (61%)
  local copies, waits for them, and re-layouts  262 us (12%)
  matrix products  221 us (10%)
  blocking collectives  168 us (8%)
  other arithmetic  154 us (7%)
    all_gather x1, waiting for transfers between devices, shards(): lax.all_gather(expert_down, 'shard', axis=1, tiled=True)  334 us
    reduce_scatter x1, waiting for transfers between devices, shards(): lax.psum_scatter(down_grad.astype(jnp.bfloat16), 'shard', scatter_dimensi...  313 us
    all_gather x1, waiting for transfers between devices, shards(): lax.all_gather(expert_up, 'shard', axis=2, tiled=True)  216 us
    unnamed x18, waiting for transfers between devices  209 us
    unnamed x143, local copies, waits for them, and re-layouts  102 us
    psum x1, waiting for transfers between devices, shards(): lax.psum(joint_grad.astype(jnp.bfloat16), 'rep').astype(jnp.float32)  93.7 us
    reduce_scatter x1, waiting for transfers between devices, shards(): lax.psum_scatter(joint_grad.astype(jnp.bfloat16), 'shard', scatter_dimens...  82.1 us
    unnamed x2, blocking collectives  75.8 us
  transfers between devices with their start and end apart: 13, of which 10 were waited for; matrix products, arithmetic and copies ran while one was open for 24% of the time, Pallas kernels for 0%

commit v1 on v0

--- a/solution.py
+++ b/solution.py
@@ -313,7 +313,7 @@
     totals = (
         lax.psum(gain_one_grad.astype(jnp.bfloat16), "rep").astype(jnp.float32),
         lax.psum(shift_one_grad.astype(jnp.bfloat16), "rep").astype(jnp.float32),
-        lax.psum(joint_grad.astype(jnp.bfloat16), "rep").astype(jnp.float32),
+        jnp.sum(lax.all_gather(joint_grad.astype(jnp.bfloat16), "rep"), axis=0).astype(jnp.float32),
         lax.psum(joint_shift_grad.astype(jnp.bfloat16), "rep").astype(jnp.float32),
         lax.psum(mixer_grad.astype(jnp.bfloat16), "rep").astype(jnp.float32),
         lax.psum(mixer_shift_grad.astype(jnp.bfloat16), "rep").astype(jnp.float32),

time: 2110 us -> 2320 us (1.100)
  waiting for transfers between devices: 1280 us -> 1480 us
    unnamed x18 -> x19, waiting for transfers between devices: 209 us -> 492 us
    reduce_scatter x1, waiting for transfers between devices: 82.1 us -> 0.02 us  [shards(): lax.psum_scatter(joint_grad.astype(jnp.bfloat16), 'shard', scatter_dimens...]
    all_gather x1, waiting for transfers between devices: 216 us -> 177 us  [shards(): lax.all_gather(expert_up, 'shard', axis=2, tiled=True)]
    unnamed x143 -> x141, local copies, waits for them, and re-layouts: 102 us -> 100 us
  transfers between devices with their start and end apart: 13 -> 14, of which waited for: 10 -> 11; matrix products, arithmetic and copies ran while one was open for 24% -> 14% of each run, Pallas kernels for 0% -> 0%
where the time goes in v1:
time: 2320 us; the launch traced here: 2310 us
  waiting for transfers between devices  1480 us (64%)
  local copies, waits for them, and re-layouts  259 us (11%)
  matrix products  218 us (9%)
  blocking collectives  185 us (8%)
  other arithmetic  156 us (7%)
    unnamed x19, waiting for transfers between devices  492 us
    all_gather x1, waiting for transfers between devices, shards(): lax.all_gather(expert_down, 'shard', axis=1, tiled=True)  334 us
    reduce_scatter x1, waiting for transfers between devices, shards(): lax.psum_scatter(down_grad.astype(jnp.bfloat16), 'shard', scatter_dimensi...  313 us
    all_gather x1, waiting for transfers between devices, shards(): lax.all_gather(expert_up, 'shard', axis=2, tiled=True)  177 us
    unnamed x141, local copies, waits for them, and re-layouts  100 us
    psum x1, waiting for transfers between devices, shards(): lax.psum(mixer_grad.astype(jnp.bfloat16), 'rep').astype(jnp.float32)  96.3 us
    unnamed x2, blocking collectives  75.9 us
    convert_element_type x1, other arithmetic, shards(): active = jax.nn.gelu(hidden, approximate=False).astype(jnp.bfloat16)  71.7 us
  transfers between devices with their start and end apart: 14, of which 11 were waited for; matrix products, arithmetic and copies ran while one was open for 14% of the time, Pallas kernels for 0%

profile of v1, /device:TPU:0, one launch (start us, length us, event | category | flops | bytes accessed | tf_op | source)
XLA Modules:
  0.0 2313.0 jit_solution(15555456939759112237)
XLA Ops:
  16.2 40.6 %all-reduce.14 = (bf16[768]{0:T(1024)(128)(2,1)S(1)}, bf16[768]{0:T(1024)(128)(2,1)S(1)}, bf16[768]{0:T(1024)(128)(2,1)S(1)}, bf16[768]{0:T(1024)(128)(2,1)S(1)}, bf16[768]{0:T(1024)(128)(2,1)S(1)}) all-reduce(bf16[768]{0:T(1024)(128)(2,1)S(1)} %dynamic-update-slice.1, ...), channel_id=1, replica_groups=mesh['shard'=8,'rep'=4] {'shard'}, use_global_device_ids=true, to_apply=%add.4 | all-reduce | flops 3840 | bytes 15360
  59.8 16.8 all-gather.1
  77.3 18.4 all-gather.2
  96.4 16.9 all-gather.3
  114.0 51.2 %all_gather.59 = bf16[4,3072]{1,0:T(4,128)(2,1)S(1)} all-gather(bf16[4,384]{1,0:T(4,128)(2,1)} %param.28), channel_id=1, replica_groups=mesh['shard'=8,'rep'=4] {'shard'}, dimensions={1}, use_global_device_ids=true | all-gather | bytes 27648 | tf_op jit(solution)/shard_map/all_gather | solution.py:154
  177.5 10.3 scatter_custom_fusion
  187.8 8.4 gather_fusion.3
  199.4 9.1 add_convert_fusion
  208.5 14.6 reshape.295
  223.1 9.3 fusion.50
  232.4 6.1 copy.163
  238.5 6.0 copy.162
  244.5 5.5 copy.164
  250.0 4.1 multiply_reduce_fusion.1
  254.2 2.9 exponential_reduce_fusion
  261.5 3.1 copy.129
  264.6 5.7 convert_element_type.192
  270.3 3.4 fusion.52
  278.5 13.3 gather_fusion.2
  292.0 8.5 gather_fusion
  300.5 5.5 fusion.49
  306.0 177.2 %all-gather.14.cloned.1.call-done = bf16[4,768,3072]{2,1,0:T(8,128)(2,1)} async-done(((bf16[4,768,384]{2,1,0:T(8,128)(2,1)}), bf16[4,768,3072]{2,1,0:T(8,128)(2,1)}) %all-gather.14.cloned.1.call-update) | async-done | bytes 18874384 | tf_op jit(solution)/shard_map/all_gather | solution.py:153
  483.1 29.5 %fusion.17 = (u8[616,3072]{1,0:T(8,128)(4,1)S(1)}, u8[616,3072]{1,0:T(8,128)(4,1)}, f32[4,616,3072]{2,1,0:T(8,128)}) fusion(f32[4,3072]{1,0:T(4,128)S(1)} %copy-done.21, bf16[4,616,768]{2,1,0:T(8,128)(2,1)} %bitcast.133, bf16[4,768,3072]{2,1,0:T(8,128)(2,1)} %all-gather.14.cloned.1.call-done), kind=kOutput, calls=%fused_computation.46 | convolution fusion | flops 11728797696 | bytes 56770560 | tf_op jit(solution)/shard_map/ecd,edf->ecf/dot_general | solution.py:158
  512.6 334.3 %all-gather.16.cloned.1.call-done = bf16[4,3072,768]{2,1,0:T(8,128)(2,1)} async-done(((bf16[4,384,768]{2,1,0:T(8,128)(2,1)}), bf16[4,3072,768]{2,1,0:T(8,128)(2,1)}) %all-gather.16.cloned.1.call-update) | async-done | bytes 18874384 | tf_op jit(solution)/shard_map/all_gather | solution.py:155
  846.9 30.0 %fusion.54 = (bf16[4,3072]{1,0:T(4,128)(2,1)}, bf16[4,616,3072]{2,1,0:T(8,128)(2,1)}) fusion(f32[4,616,3072]{2,1,0:T(8,128)} %get-tuple-element.71, f32[4,3072]{1,0:T(4,128)S(1)} %copy-done.21, bf16[4,616,768]{2,1,0:T(8,128)(2,1)} %get-tuple-element.54, bf16[4,3072,768]{2,1,0:T(8,128)(2,1)} %all-gather.16.cloned.1.call-done), kind=kOutput, calls=%fused_computation.148 | convolution fusion | flops 11717431296 | bytes 68149248 | tf_op jit(solution)/shard_map/ecd,efd->ecf/dot_general | solution.py:189
  876.9 19.8 fusion.55
  896.7 13.7 gather_fusion.4
  910.4 8.3 reshape.192
  918.7 11.5 reduce_sum.279
  930.3 71.7 %fusion.2 = bf16[4,616,3072]{2,1,0:T(8,128)(2,1)} fusion(f32[4,616,3072]{2,1,0:T(8,128)} %get-tuple-element.71, f32[4,3072]{1,0:T(4,128)S(1)} %copy-done.21, u8[616,3072]{1,0:T(8,128)(4,1)} %get-tuple-element.16, u8[616,3072]{1,0:T(8,128)(4,1)S(1)} %get-tuple-element.15), kind=kLoop, calls=%fused_computation.10 | loop fusion | flops 537427968 | bytes 49250304 | tf_op jit(solution)/shard_map/convert_element_type | solution.py:161
  1002.0 20.5 broadcast_add_fusion
  1022.5 13.8 gather_fusion.1
  1036.3 8.0 reshape.189
  1044.3 17.1 multiply_reduce_fusion.2
  1064.8 5.4 multiply_reduce_fusion.4
  1074.8 4.4 reshape.296
  1079.2 5.0 copy.138
  1084.2 8.3 convert_bitcast_fusion
  1092.5 9.1 multiply_reduce_fusion
  1101.6 6.8 multiply_convert_fusion
  1113.8 8.8 copy.143
  1122.6 13.9 convert_element_type.207
  1136.6 8.4 convolution_convert_fusion.2
  1145.1 24.3 %convolution_convert_fusion.1 = bf16[4,768,3072]{2,1,0:T(8,128)(2,1)} fusion(bf16[4,616,768]{2,1,0:T(8,128)(2,1)} %bitcast.134, bf16[4,616,3072]{2,1,0:T(8,128)(2,1)} %get-tuple-element.77), kind=kOutput, calls=%fused_computation.41 | convolution fusion | flops 11636047872 | bytes 37797888 | tf_op jit(solution)/shard_map/ecd,ecf->edf/dot_general | solution.py:196
  1169.4 29.6 %copy.152 = bf16[4,768,3072]{1,0,2:T(4,128)(2,1)} copy(bf16[4,768,3072]{2,1,0:T(8,128)(2,1)} %convolution_convert_fusion.1) | data formatting | bytes 37748736
  1199.0 20.0 copy.167
  1219.1 4.7 convolution_convert_fusion.4
  1223.9 21.9 convolution_convert_fusion
  1255.5 282.2 %reduce-scatter.29.cloned.1.call-done = bf16[384,3072]{1,0:T(8,128)(2,1)} async-done(((bf16[3072,3072]{1,0:T(8,128)(2,1)}), bf16[384,3072]{1,0:T(8,128)(2,1)}) %reduce-scatter.29.cloned.1.call-update) | async-done | bytes 2359312
  1537.7 5.8 reshape.285
  1543.4 5.4 copy.153
  1548.8 56.2 %reduce-scatter.21.cloned.1.call-done = bf16[96,768]{1,0:T(8,128)(2,1)} async-done(((bf16[768,768]{1,0:T(8,128)(2,1)}), bf16[96,768]{1,0:T(8,128)(2,1)}) %reduce-scatter.21.cloned.1.call-update) | async-done | bytes 147472 | tf_op jit(solution)/shard_map/reduce_scatter | solution.py:282
  1605.0 312.7 %reduce-scatter.23.cloned.1.call-done = bf16[4,384,768]{2,1,0:T(8,128)(2,1)} async-done(((bf16[4,3072,768]{2,1,0:T(8,128)(2,1)}), bf16[4,384,768]{2,1,0:T(8,128)(2,1)}) %reduce-scatter.23.cloned.1.call-update) | async-done | bytes 2359312 | tf_op jit(solution)/shard_map/reduce_scatter | solution.py:208
  1918.4 63.7 %reduce-scatter.33.cloned.1.call-done = bf16[96,4]{1,0:T(8,128)(2,1)} async-done(((bf16[768,4]{1,0:T(8,128)(2,1)}), bf16[96,4]{1,0:T(8,128)(2,1)}) %reduce-scatter.33.cloned.1.call-update) | async-done | bytes 784
  1982.8 9.8 multiply_reduce_fusion.5
  1992.6 35.2 %all-reduce.13 = (bf16[768]{0:T(1024)(128)(2,1)S(1)}, bf16[768]{0:T(1024)(128)(2,1)S(1)}, bf16[768]{0:T(1024)(128)(2,1)S(1)}, bf16[768]{0:T(1024)(128)(2,1)S(1)}, bf16[768]{0:T(1024)(128)(2,1)S(1)}) all-reduce(bf16[768]{0:T(1024)(128)(2,1)S(1)} %get-tuple-element.19, ...), channel_id=3, replica_groups=mesh['shard'=8,'rep'=4] {'shard'}, use_global_device_ids=true, to_apply=%region_24.25.clone | all-reduce | flops 3840 | bytes 15360
  2028.2 4.4 multiply_add_fusion
  2032.7 14.2 reduce-scatter.25.cloned.1.call-done
  2047.7 63.5 %reduce-scatter.27.cloned.1.call-done = bf16[96,4]{1,0:T(8,128)(2,1)} async-done(((bf16[768,4]{1,0:T(8,128)(2,1)}), bf16[96,4]{1,0:T(8,128)(2,1)}) %reduce-scatter.27.cloned.1.call-update) | async-done | bytes 784
  2112.0 65.3 %reduce-scatter.31.cloned.1.call-done = bf16[384,4]{1,0:T(8,128)(2,1)} async-done(((bf16[3072,4]{1,0:T(8,128)(2,1)}), bf16[384,4]{1,0:T(8,128)(2,1)}) %reduce-scatter.31.cloned.1.call-update) | async-done | bytes 3088
  2178.2 5.8 all-reduce.15
  2188.9 9.7 all-gather.18.cloned.1.call-done
  2201.4 96.3 %all-reduce.19.cloned.1.call-done = (bf16[96,768]{1,0:T(8,128)(2,1)}, bf16[4,768,384]{2,1,0:T(8,128)(2,1)}, bf16[4,384,768]{2,1,0:T(8,128)(2,1)}) async-done(((bf16[96,768]{1,0:T(8,128)(2,1)}, bf16[4,768,384]{2,1,0:T(8,128)(2,1)}, bf16[4,384,768]{2,1,0:T(8,128)(2,1)}), (bf16[96,768]{1,0:T(8,128)(2,1)}, bf16[4,768,384]{2,1,0:T(8,128)(2,1)}, bf16[4,384,768]{2,1,0:T(8,128)(2,1)})) %all-reduce.19.cloned.1.call-update) | async-done | bytes 4866064 | tf_op jit(solution)/shard_map/psum | solution.py:318
  2299.5 4.2 convert_element_type.227
  (247 shorter events, 76.6 us)
Async XLA Ops:
  7.2 168.0 %copy-start.6 = (f32[985,768]{1,0:T(8,128)S(1)}, f32[985,768]{1,0:T(8,128)}, u32[]{:S(2)}) copy-start(f32[985,768]{1,0:T(8,128)} %param.16) | copy-start | bytes 9077764
  7.2 192.2 %all-gather.10.cloned.1.call-start = ((), (), s32[]{:S(2)}) async-start(), calls=%async_computation.8 | async-start | bytes 3981312 | tf_op jit(solution)/shard_map/all_gather | solution.py:87
  7.9 262.4 %all-gather.12.cloned.1.call-start = ((), (), s32[]{:S(2)}) async-start(), calls=%async_computation.9 | async-start | bytes 1327104 | tf_op jit(solution)/shard_map/all_gather | solution.py:89
  8.7 474.4 %all-gather.14.cloned.1.call-start = ((), (), s32[]{:S(2)}) async-start(), calls=%async_computation.10 | async-start | bytes 21233664 | tf_op jit(solution)/shard_map/all_gather | solution.py:153
  9.4 837.5 %all-gather.16.cloned.1.call-start = ((), (), s32[]{:S(2)}) async-start(), calls=%async_computation.11 | async-start | bytes 21233664 | tf_op jit(solution)/shard_map/all_gather | solution.py:155
  10.0 1244.7 %reduce-scatter.19.cloned.1.call-start = ((), (), s32[]{:S(2)}) async-start(), calls=%async_computation.12 | async-start | bytes 3981312 | tf_op jit(solution)/shard_map/reduce_scatter | solution.py:276
  172.6 4.8 copy-start.26
  172.6 4.8 copy-start.36
  187.8 9.1 copy-start.39
  187.8 11.6 copy-start.40
  187.8 11.6 copy-start.46
  196.9 11.6 copy-start.34
  199.4 9.1 copy-start.42
  250.0 4.1 copy-start.3
  254.2 4.8 copy-start
  254.2 4.8 copy-start.11
  259.0 2.5 copy-start.18
  261.4 8.9 copy-start.7
  261.4 8.9 copy-start.48
  270.3 5.1 copy-start.28
  270.3 5.1 copy-start.44
  273.7 1.6 copy-start.1
  273.7 2.2 copy-start.33
  273.7 3.4 copy-start.22
  273.8 2.8 copy-start.23
  275.4 1.2 copy-start.30
  275.9 16.0 copy-start.10
  277.4 0.8 copy-start.15
  300.5 182.7 %copy-start.21 = (f32[4,3072]{1,0:T(4,128)S(1)}, f32[4,3072]{1,0:T(4,128)}, u32[]{:S(2)}) copy-start(f32[4,3072]{1,0:T(4,128)} %convert_element_type.198) | copy-start | bytes 147460
  876.9 19.8 copy-start.27
  930.3 71.7 %copy-start.45 = (f32[768,4]{0,1:T(4,128)S(1)}, f32[768,4]{0,1:T(4,128)}, u32[]{:S(2)}) copy-start(f32[768,4]{0,1:T(4,128)} %reshape.279) | copy-start | bytes 36868
  1036.3 8.0 copy-start.16
  1044.3 20.5 copy-start.2
  1064.8 5.5 copy-start.5
  1064.8 5.5 copy-start.24
  1064.8 5.5 copy-start.29
  1064.8 5.5 copy-start.31
  1070.3 3.1 copy-start.49
  1071.8 1.6 copy-start.13
  1074.8 9.4 copy-start.19
  1084.2 8.3 copy-start.12
  1084.2 17.4 slice-start
  1084.2 17.4 slice-start.1
  1092.5 9.1 slice-start.2
  1101.6 6.8 copy-start.9
  1108.4 2.1 copy-start.4
  1110.5 1.6 copy-start.14
  1122.6 14.0 copy-start.8
  1122.6 14.0 copy-start.35
  1122.6 14.0 copy-start.41
  1122.6 14.0 copy-start.43
  1122.6 14.0 copy-start.47
  1145.1 392.6 %reduce-scatter.29.cloned.1.call-start = ((), (), s32[]{:S(2)}) async-start(), calls=%async_computation.18 | async-start | bytes 21233664
  1219.1 386.0 %reduce-scatter.21.cloned.1.call-start = ((), (), s32[]{:S(2)}) async-start(), calls=%async_computation.13 | async-start | bytes 1327104 | tf_op jit(solution)/shard_map/reduce_scatter | solution.py:282
  1223.9 693.8 %reduce-scatter.23.cloned.1.call-start = ((), (), s32[]{:S(2)}) async-start(), calls=%async_computation.14 | async-start | bytes 21233664 | tf_op jit(solution)/shard_map/reduce_scatter | solution.py:208
  1245.8 0.7 copy-start.37
  1245.8 7.6 copy-start.38
  1245.8 736.2 %reduce-scatter.33.cloned.1.call-start = ((), (), s32[]{:S(2)}) async-start(), calls=%async_computation.20 | async-start | bytes 221184
  1247.4 799.5 %reduce-scatter.25.cloned.1.call-start = ((), (), s32[]{:S(2)}) async-start(), calls=%async_computation.16 | async-start | bytes 221184
  1250.7 860.4 %reduce-scatter.27.cloned.1.call-start = ((), (), s32[]{:S(2)}) async-start(), calls=%async_computation.17 | async-start | bytes 221184
  1253.4 923.9 %reduce-scatter.31.cloned.1.call-start = ((), (), s32[]{:S(2)}) async-start(), calls=%async_computation.19 | async-start | bytes 884736
  1254.7 944.0 %all-gather.18.cloned.1.call-start = ((), (), s32[]{:S(2)}) async-start(), calls=%async_computation.15 | async-start | bytes 2211840 | tf_op jit(solution)/shard_map/all_gather | solution.py:316
  1255.4 1042.3 %all-reduce.19.cloned.1.call-start = ((), (), s32[]{:S(2)}) async-start(), calls=%async_computation.21 | async-start | bytes 9732096 | tf_op jit(solution)/shard_map/psum | solution.py:318
  2297.7 6.0 copy-start.17
  (3 other events, 1.8 us)
Sparse Core Ops, SparseCore 0:
  10.2 67.7 all-gather.9
  80.2 40.0 all-gather.11
  121.8 361.2 all-gather.13
  484.5 362.3 all-gather.15
  1145.2 79.3 reduce-scatter.18
  1228.3 309.2 reduce-scatter.28
  1541.1 63.9 reduce-scatter.20
  1608.9 308.7 reduce-scatter.22
  1920.9 61.0 reduce-scatter.32
  1985.7 61.0 reduce-scatter.24
  2050.1 60.9 reduce-scatter.26
  2114.9 62.3 reduce-scatter.30
  2178.8 19.7 all-gather.17
  2201.0 96.6 all-reduce.18
